TPU v7x, 512 devices: a whole 4x4x16 slice. The times are simulated.
512 devices in a mesh: ctx: 32 (over z, core), tp: 16 (over x, y).
Axes of the slice: x: 4, y: 4, z: 16, core: 2. Of those that a mesh axis runs over, the one named last changes fastest.
Arguments:
- queries: bfloat16 [8192, 8192], P('ctx', 'tp'), may hold values from -6 to 6
- keys: bfloat16 [8192, 8192], P('ctx', 'tp'), may hold values from -0.0625 to 0.0625
- values: bfloat16 [8192, 8192], P('ctx', 'tp'), may hold values from -6 to 6
- log_keep: float32 [64, 8192], P('tp', 'ctx'), may hold values from -1 to 0, as said below
- state_in: float32 [64, 128, 128], P('tp'), may hold values from -6 to 6
- norm_gain: float32 [8192], P('tp'), may hold values from 0.1 to 1.9
- out_weight: bfloat16 [8192, 6144], P('tp', 'ctx'), may hold values from -0.125 to 0.125
Outputs:
- normed: bfloat16 [8192, 8192], P('ctx', 'tp')
- state_out: float32 [64, 128, 128], P('tp', 'ctx')
- layer_out: bfloat16 [8192, 6144], P('ctx', 'tp')
Inputs may be any that keep to these rules, and one draw needn't show every extreme that they name: `log_keep`: every entry is a logarithm of a keep factor, so at most 0.
All inputs are finite; a program needn't handle non-finite values.
Results may differ from a plain program's by a relative error of at most 0.014.
Values may be sent and summed in bfloat16 or wider, within the bound.
No kernel may reach another device: no remote copies, remote signals or barrier semaphores. Data moves between devices by JAX's collectives and lax.ppermute only.
A program may use at most 64 MiB of HBM per device.

v0:
```python
import jax
import jax.numpy as jnp
from jax import lax
from jax.sharding import PartitionSpec as P

H = 64
DH = 128
SPAN = 256
HIGH = lax.Precision.HIGHEST
EPSILON = 1e-06


def shifted(x, axis, by):
    peers = lax.axis_size(axis)
    pairs = [(i, i + by) for i in range(peers) if 0 <= i + by < peers]
    return lax.ppermute(x, axis, pairs)


def broadcast(x, axis, root):
    mine = lax.axis_index(axis) == root
    return lax.psum(jnp.where(mine, x, jnp.zeros_like(x)), axis)


def join_states(earlier, later):
    log_early, state_early = earlier
    log_late, state_late = later
    return (log_early + log_late, jnp.exp(log_late)[:, None, None] * state_early + state_late)


def close_chain(prev_log, prev_state, own_log, own_state, state_in):
    last_log, last_state = join_states((prev_log, prev_state), (own_log, own_state))
    return jnp.exp(last_log)[:, None, None] * state_in + last_state


def per_device(queries, keys, values, log_keep, state_in, norm_gain, out_weight):
    tokens_here = queries.shape[0]
    heads = log_keep.shape[0]
    width = state_in.shape[1]
    blocks = tokens_here // SPAN
    q_blocks = queries.reshape(blocks, SPAN, heads, width)
    k_blocks = keys.reshape(blocks, SPAN, heads, width)
    v_blocks = values.reshape(blocks, SPAN, heads, width)
    within = jnp.cumsum(log_keep.reshape(heads, blocks, SPAN), axis=2)
    causal = jnp.tril(jnp.ones((SPAN, SPAN), dtype=bool))
    spread = within[:, :, :, None] - within[:, :, None, :]
    decay = jnp.where(causal, jnp.exp(jnp.minimum(spread, 0.0)), 0.0)
    scores = jnp.einsum("cshd,cthd->hcst", q_blocks, k_blocks, preferred_element_type=jnp.float32)
    weights = (scores * decay).astype(jnp.bfloat16)
    intra = jnp.einsum("hcst,cthd->cshd", weights, v_blocks, preferred_element_type=jnp.float32)
    block_log = within[:, :, -1]
    key_factor = jnp.exp(block_log[:, :, None] - within).transpose(1, 2, 0)
    keys_decayed = (k_blocks * key_factor[:, :, :, None]).astype(jnp.bfloat16)
    increments = jnp.einsum(
        "cshd,cshe->chde", keys_decayed, v_blocks, preferred_element_type=jnp.float32
    )
    running = jnp.cumsum(block_log, axis=1)
    preceding_blocks = running - block_log
    order = jnp.arange(blocks)
    earlier_mask = order[None, :] < order[:, None]
    relative = preceding_blocks[:, :, None] - running[:, None, :]
    mixing = jnp.where(earlier_mask[None], jnp.exp(jnp.minimum(relative, 0.0)), 0.0)
    local_prefix = jnp.einsum("hcx,xhde->chde", mixing, increments, precision=HIGH)
    own_log = running[:, -1]
    own_state = jnp.einsum(
        "hc,chde->hde", jnp.exp(own_log[:, None] - running), increments, precision=HIGH
    )
    sequence_parts = lax.axis_size("ctx")
    zero_log = jnp.zeros_like(own_log)
    zero_state = jnp.zeros_like(own_state)

    def cycle_step(turn, carry):
        passed = join_states(carry, (own_log, own_state))
        return shifted((passed[0], passed[1]), "ctx", 1)

    prev_log, prev_state = lax.fori_loop(0, sequence_parts - 1, cycle_step, (zero_log, zero_state))
    closing = close_chain(prev_log, prev_state, own_log, own_state, state_in)
    shared_final = broadcast(closing, "ctx", sequence_parts - 1)
    share_rows = width // sequence_parts
    row_start = lax.axis_index("ctx") * share_rows
    final_share = lax.dynamic_slice_in_dim(shared_final, row_start, share_rows, 1)
    incoming_state = jnp.exp(prev_log)[:, None, None] * state_in + prev_state
    starts = jnp.exp(preceding_blocks).T[:, :, None, None] * incoming_state[None] + local_prefix
    starts_low = starts.astype(jnp.bfloat16)
    inter = jnp.einsum("cshd,chde->cshe", q_blocks, starts_low, preferred_element_type=jnp.float32)
    inter = inter * jnp.exp(within).transpose(1, 2, 0)[:, :, :, None]
    attended = (intra + inter).reshape(tokens_here, heads * width)
    squares = lax.psum(jnp.sum(attended * attended, axis=1), "tp")
    scale = lax.rsqrt(squares / (H * DH) + EPSILON)
    normed = (attended * scale[:, None] * norm_gain).astype(jnp.bfloat16)
    partials = jnp.dot(
        normed,
        lax.all_gather(out_weight, "ctx", axis=1, tiled=True),
        preferred_element_type=jnp.float32,
    )
    layer_out = lax.psum_scatter(
        partials.astype(jnp.bfloat16), "tp", scatter_dimension=1, tiled=True
    )
    return (normed, final_share, layer_out)


def solution(mesh):
    return jax.shard_map(
        per_device,
        mesh=mesh,
        in_specs=(
            P("ctx", "tp"),
            P("ctx", "tp"),
            P("ctx", "tp"),
            P("tp", "ctx"),
            P("tp", None, None),
            P("tp"),
            P("tp", "ctx"),
        ),
        out_specs=(P("ctx", "tp"), P("tp", "ctx", None), P("ctx", "tp")),
        check_vma=False,
    )
```

profile of v0, /device:TPU:2, one launch (start us, length us, event | category | flops | bytes accessed | tf_op | source)
XLA Modules:
  0.0 631.8 jit_solution(6297971191016926080)
XLA Ops:
  12.8 288.4 %while.13 = (s32[]{:T(128)}, f32[4]{0:T(128)S(1)}, f32[4,128,128]{2,1,0:T(8,128)S(1)}, f32[4]{0:T(128)S(1)}, f32[4,1,1]{0,2,1:T(1,128)S(1)}, /*index=5*/f32[4,128,128]{2,1,0:T(8,128)S(1)}, s32[]{:T(128)}) while((s32[]{:T(128)}, f32[4]{0:T(128)S(1)}, f32[4,128,128]{2,1,0:T(8,128)S(1)}, f32[4]{0:T(128)S(1)}, f32[4,1,1]{0,2,1:T(1,128)S(1)}, ...), condition=%wide.region_3.4_spmd, body=%wide.region_2.3_spmd.sunk | while | flops 131078 | bytes 1835293 | solution.py:75
  14.7 4.1 collective-permute-start
  19.7 2.5 collective-permute-start.1
  22.2 4.4 collective-permute-start
  30.1 4.4 collective-permute-start
  35.4 2.5 collective-permute-start.1
  38.0 4.4 collective-permute-start
  43.3 7.2 %collective-permute-start.1 = (f32[4,128,128]{2,1,0:T(8,128)S(1)}, f32[4,128,128]{2,1,0:T(8,128)S(1)}, u32[]{:S(2)}, u32[]{:S(2)}) collective-permute-start(f32[4,128,128]{2,1,0:T(8,128)S(1)} %multiply_add_fusion.2), channel_id=1, source_target_pairs={{0,16},{16,32},{32,48},{48,64},{64,80},{80,96},{96,112},{112,128},... | collective-permute-start | bytes 786440 | tf_op jit(solution)/shard_map/while/body/eval_jaxpr/ppermute | solution.py:16
  50.6 4.4 collective-permute-start
  55.9 7.1 %collective-permute-start.1 = (f32[4,128,128]{2,1,0:T(8,128)S(1)}, f32[4,128,128]{2,1,0:T(8,128)S(1)}, u32[]{:S(2)}, u32[]{:S(2)}) collective-permute-start(f32[4,128,128]{2,1,0:T(8,128)S(1)} %multiply_add_fusion.2), channel_id=1, source_target_pairs={{0,16},{16,32},{32,48},{48,64},{64,80},{80,96},{96,112},{112,128},... | collective-permute-start | bytes 786440 | tf_op jit(solution)/shard_map/while/body/eval_jaxpr/ppermute | solution.py:16
  63.0 4.5 collective-permute-start
  68.4 7.0 %collective-permute-start.1 = (f32[4,128,128]{2,1,0:T(8,128)S(1)}, f32[4,128,128]{2,1,0:T(8,128)S(1)}, u32[]{:S(2)}, u32[]{:S(2)}) collective-permute-start(f32[4,128,128]{2,1,0:T(8,128)S(1)} %multiply_add_fusion.2), channel_id=1, source_target_pairs={{0,16},{16,32},{32,48},{48,64},{64,80},{80,96},{96,112},{112,128},... | collective-permute-start | bytes 786440 | tf_op jit(solution)/shard_map/while/body/eval_jaxpr/ppermute | solution.py:16
  75.4 4.5 collective-permute-start
  80.8 4.7 collective-permute-start.1
  85.4 4.5 collective-permute-start
  90.8 2.9 collective-permute-start.1
  93.7 4.5 collective-permute-start
  99.1 4.4 collective-permute-start.1
  103.5 5.9 collective-permute-start
  110.3 2.5 collective-permute-start.1
  112.9 5.6 collective-permute-start
  119.4 2.5 collective-permute-start.1
  121.9 5.6 collective-permute-start
  128.5 2.5 collective-permute-start.1
  131.0 5.6 collective-permute-start
  140.1 5.6 collective-permute-start
  149.2 5.6 collective-permute-start
  158.3 5.6 collective-permute-start
  167.4 5.6 collective-permute-start
  176.5 5.6 collective-permute-start
  185.6 5.6 collective-permute-start
  194.7 5.6 collective-permute-start
  203.8 5.6 collective-permute-start
  212.9 5.6 collective-permute-start
  221.9 5.6 collective-permute-start
  231.0 5.6 collective-permute-start
  240.1 5.6 collective-permute-start
  249.2 5.6 collective-permute-start
  258.3 5.6 collective-permute-start
  267.4 5.6 collective-permute-start
  276.5 5.6 collective-permute-start
  285.6 5.6 collective-permute-start
  294.7 5.6 collective-permute-start
  303.5 36.8 %psum.14 = f32[256]{0:T(256)S(1)} all-reduce(f32[256]{0:T(256)S(1)} %get-tuple-element.79), channel_id=1, replica_groups=mesh['ctx'=32,'tp'=16] {'tp'}, use_global_device_ids=true, to_apply=%region_5.6 | all-reduce | flops 256 | bytes 2048 | tf_op jit(solution)/shard_map/psum | solution.py:87
  341.1 4.7 convolution_convert_fusion
  345.8 2.8 copy.38
  348.6 178.8 %all-reduce.2.cloned.1.call-done = f32[4,128,128]{2,1,0:T(8,128)} async-done(((f32[4,128,128]{2,1,0:T(8,128)}), f32[4,128,128]{2,1,0:T(8,128)}) %all-reduce.2.cloned.1.call-update) | async-done | bytes 262160 | tf_op jit(solution)/shard_map/psum | solution.py:21
  528.7 94.8 %reduce-scatter.4.cloned.1.call-done = bf16[384,256]{1,0:T(8,128)(2,1)} async-done(((bf16[6144,256]{1,0:T(8,128)(2,1)}), bf16[384,256]{1,0:T(8,128)(2,1)}) %reduce-scatter.4.cloned.1.call-update) | async-done | bytes 196624
  (189 shorter events, 89.3 us)
Async XLA Ops:
  7.2 333.9 %all-gather.2.cloned.1.call-start = ((), (), s32[]{:S(2)}) async-start(), calls=%async_computation.2 | async-start | bytes 6488064 | tf_op jit(solution)/shard_map/all_gather | solution.py:92
  7.9 519.5 %all-reduce.2.cloned.1.call-start = ((), (), s32[]{:S(2)}) async-start(), calls=%async_computation.1 | async-start | bytes 524288 | tf_op jit(solution)/shard_map/psum | solution.py:21
  12.9 6.7 %collective-permute-start.1 = (f32[4,128,128]{2,1,0:T(8,128)S(1)}, f32[4,128,128]{2,1,0:T(8,128)S(1)}, u32[]{:S(2)}, u32[]{:S(2)}) collective-permute-start(f32[4,128,128]{2,1,0:T(8,128)S(1)} %multiply_add_fusion.2), channel_id=1, source_target_pairs={{0,16},{16,32},{32,48},{48,64},{64,80},{80,96},{96,112},{112,128},... | collective-permute-start | bytes 786440 | tf_op jit(solution)/shard_map/while/body/eval_jaxpr/ppermute | solution.py:16
  19.7 7.8 %collective-permute-start.1 = (f32[4,128,128]{2,1,0:T(8,128)S(1)}, f32[4,128,128]{2,1,0:T(8,128)S(1)}, u32[]{:S(2)}, u32[]{:S(2)}) collective-permute-start(f32[4,128,128]{2,1,0:T(8,128)S(1)} %multiply_add_fusion.2), channel_id=1, source_target_pairs={{0,16},{16,32},{32,48},{48,64},{64,80},{80,96},{96,112},{112,128},... | collective-permute-start | bytes 786440 | tf_op jit(solution)/shard_map/while/body/eval_jaxpr/ppermute | solution.py:16
  27.5 7.8 %collective-permute-start.1 = (f32[4,128,128]{2,1,0:T(8,128)S(1)}, f32[4,128,128]{2,1,0:T(8,128)S(1)}, u32[]{:S(2)}, u32[]{:S(2)}) collective-permute-start(f32[4,128,128]{2,1,0:T(8,128)S(1)} %multiply_add_fusion.2), channel_id=1, source_target_pairs={{0,16},{16,32},{32,48},{48,64},{64,80},{80,96},{96,112},{112,128},... | collective-permute-start | bytes 786440 | tf_op jit(solution)/shard_map/while/body/eval_jaxpr/ppermute | solution.py:16
  35.4 7.8 %collective-permute-start.1 = (f32[4,128,128]{2,1,0:T(8,128)S(1)}, f32[4,128,128]{2,1,0:T(8,128)S(1)}, u32[]{:S(2)}, u32[]{:S(2)}) collective-permute-start(f32[4,128,128]{2,1,0:T(8,128)S(1)} %multiply_add_fusion.2), channel_id=1, source_target_pairs={{0,16},{16,32},{32,48},{48,64},{64,80},{80,96},{96,112},{112,128},... | collective-permute-start | bytes 786440 | tf_op jit(solution)/shard_map/while/body/eval_jaxpr/ppermute | solution.py:16
  43.3 12.5 %collective-permute-start.1 = (f32[4,128,128]{2,1,0:T(8,128)S(1)}, f32[4,128,128]{2,1,0:T(8,128)S(1)}, u32[]{:S(2)}, u32[]{:S(2)}) collective-permute-start(f32[4,128,128]{2,1,0:T(8,128)S(1)} %multiply_add_fusion.2), channel_id=1, source_target_pairs={{0,16},{16,32},{32,48},{48,64},{64,80},{80,96},{96,112},{112,128},... | collective-permute-start | bytes 786440 | tf_op jit(solution)/shard_map/while/body/eval_jaxpr/ppermute | solution.py:16
  55.9 12.4 %collective-permute-start.1 = (f32[4,128,128]{2,1,0:T(8,128)S(1)}, f32[4,128,128]{2,1,0:T(8,128)S(1)}, u32[]{:S(2)}, u32[]{:S(2)}) collective-permute-start(f32[4,128,128]{2,1,0:T(8,128)S(1)} %multiply_add_fusion.2), channel_id=1, source_target_pairs={{0,16},{16,32},{32,48},{48,64},{64,80},{80,96},{96,112},{112,128},... | collective-permute-start | bytes 786440 | tf_op jit(solution)/shard_map/while/body/eval_jaxpr/ppermute | solution.py:16
  68.4 12.3 %collective-permute-start.1 = (f32[4,128,128]{2,1,0:T(8,128)S(1)}, f32[4,128,128]{2,1,0:T(8,128)S(1)}, u32[]{:S(2)}, u32[]{:S(2)}) collective-permute-start(f32[4,128,128]{2,1,0:T(8,128)S(1)} %multiply_add_fusion.2), channel_id=1, source_target_pairs={{0,16},{16,32},{32,48},{48,64},{64,80},{80,96},{96,112},{112,128},... | collective-permute-start | bytes 786440 | tf_op jit(solution)/shard_map/while/body/eval_jaxpr/ppermute | solution.py:16
  80.8 10.0 %collective-permute-start.1 = (f32[4,128,128]{2,1,0:T(8,128)S(1)}, f32[4,128,128]{2,1,0:T(8,128)S(1)}, u32[]{:S(2)}, u32[]{:S(2)}) collective-permute-start(f32[4,128,128]{2,1,0:T(8,128)S(1)} %multiply_add_fusion.2), channel_id=1, source_target_pairs={{0,16},{16,32},{32,48},{48,64},{64,80},{80,96},{96,112},{112,128},... | collective-permute-start | bytes 786440 | tf_op jit(solution)/shard_map/while/body/eval_jaxpr/ppermute | solution.py:16
  90.8 8.2 %collective-permute-start.1 = (f32[4,128,128]{2,1,0:T(8,128)S(1)}, f32[4,128,128]{2,1,0:T(8,128)S(1)}, u32[]{:S(2)}, u32[]{:S(2)}) collective-permute-start(f32[4,128,128]{2,1,0:T(8,128)S(1)} %multiply_add_fusion.2), channel_id=1, source_target_pairs={{0,16},{16,32},{32,48},{48,64},{64,80},{80,96},{96,112},{112,128},... | collective-permute-start | bytes 786440 | tf_op jit(solution)/shard_map/while/body/eval_jaxpr/ppermute | solution.py:16
  99.1 11.1 %collective-permute-start.1 = (f32[4,128,128]{2,1,0:T(8,128)S(1)}, f32[4,128,128]{2,1,0:T(8,128)S(1)}, u32[]{:S(2)}, u32[]{:S(2)}) collective-permute-start(f32[4,128,128]{2,1,0:T(8,128)S(1)} %multiply_add_fusion.2), channel_id=1, source_target_pairs={{0,16},{16,32},{32,48},{48,64},{64,80},{80,96},{96,112},{112,128},... | collective-permute-start | bytes 786440 | tf_op jit(solution)/shard_map/while/body/eval_jaxpr/ppermute | solution.py:16
  103.5 6.7 %collective-permute-start = (f32[4]{0:T(128)S(1)}, f32[4]{0:T(128)S(1)}, u32[]{:S(2)}, u32[]{:S(2)}) collective-permute-start(f32[4]{0:T(128)S(1)} %add.76), channel_id=1, source_target_pairs={{0,16},{16,32},{32,48},{48,64},{64,80},{80,96},{96,112},{112,128},... | collective-permute-start | bytes 56 | tf_op jit(solution)/shard_map/while/body/eval_jaxpr/ppermute | solution.py:16
  110.3 9.0 %collective-permute-start.1 = (f32[4,128,128]{2,1,0:T(8,128)S(1)}, f32[4,128,128]{2,1,0:T(8,128)S(1)}, u32[]{:S(2)}, u32[]{:S(2)}) collective-permute-start(f32[4,128,128]{2,1,0:T(8,128)S(1)} %multiply_add_fusion.2), channel_id=1, source_target_pairs={{0,16},{16,32},{32,48},{48,64},{64,80},{80,96},{96,112},{112,128},... | collective-permute-start | bytes 786440 | tf_op jit(solution)/shard_map/while/body/eval_jaxpr/ppermute | solution.py:16
  112.9 6.4 %collective-permute-start = (f32[4]{0:T(128)S(1)}, f32[4]{0:T(128)S(1)}, u32[]{:S(2)}, u32[]{:S(2)}) collective-permute-start(f32[4]{0:T(128)S(1)} %add.76), channel_id=1, source_target_pairs={{0,16},{16,32},{32,48},{48,64},{64,80},{80,96},{96,112},{112,128},... | collective-permute-start | bytes 56 | tf_op jit(solution)/shard_map/while/body/eval_jaxpr/ppermute | solution.py:16
  119.4 9.0 %collective-permute-start.1 = (f32[4,128,128]{2,1,0:T(8,128)S(1)}, f32[4,128,128]{2,1,0:T(8,128)S(1)}, u32[]{:S(2)}, u32[]{:S(2)}) collective-permute-start(f32[4,128,128]{2,1,0:T(8,128)S(1)} %multiply_add_fusion.2), channel_id=1, source_target_pairs={{0,16},{16,32},{32,48},{48,64},{64,80},{80,96},{96,112},{112,128},... | collective-permute-start | bytes 786440 | tf_op jit(solution)/shard_map/while/body/eval_jaxpr/ppermute | solution.py:16
  121.9 6.4 %collective-permute-start = (f32[4]{0:T(128)S(1)}, f32[4]{0:T(128)S(1)}, u32[]{:S(2)}, u32[]{:S(2)}) collective-permute-start(f32[4]{0:T(128)S(1)} %add.76), channel_id=1, source_target_pairs={{0,16},{16,32},{32,48},{48,64},{64,80},{80,96},{96,112},{112,128},... | collective-permute-start | bytes 56 | tf_op jit(solution)/shard_map/while/body/eval_jaxpr/ppermute | solution.py:16
  128.5 9.0 %collective-permute-start.1 = (f32[4,128,128]{2,1,0:T(8,128)S(1)}, f32[4,128,128]{2,1,0:T(8,128)S(1)}, u32[]{:S(2)}, u32[]{:S(2)}) collective-permute-start(f32[4,128,128]{2,1,0:T(8,128)S(1)} %multiply_add_fusion.2), channel_id=1, source_target_pairs={{0,16},{16,32},{32,48},{48,64},{64,80},{80,96},{96,112},{112,128},... | collective-permute-start | bytes 786440 | tf_op jit(solution)/shard_map/while/body/eval_jaxpr/ppermute | solution.py:16
  131.0 6.4 %collective-permute-start = (f32[4]{0:T(128)S(1)}, f32[4]{0:T(128)S(1)}, u32[]{:S(2)}, u32[]{:S(2)}) collective-permute-start(f32[4]{0:T(128)S(1)} %add.76), channel_id=1, source_target_pairs={{0,16},{16,32},{32,48},{48,64},{64,80},{80,96},{96,112},{112,128},... | collective-permute-start | bytes 56 | tf_op jit(solution)/shard_map/while/body/eval_jaxpr/ppermute | solution.py:16
  137.6 9.0 %collective-permute-start.1 = (f32[4,128,128]{2,1,0:T(8,128)S(1)}, f32[4,128,128]{2,1,0:T(8,128)S(1)}, u32[]{:S(2)}, u32[]{:S(2)}) collective-permute-start(f32[4,128,128]{2,1,0:T(8,128)S(1)} %multiply_add_fusion.2), channel_id=1, source_target_pairs={{0,16},{16,32},{32,48},{48,64},{64,80},{80,96},{96,112},{112,128},... | collective-permute-start | bytes 786440 | tf_op jit(solution)/shard_map/while/body/eval_jaxpr/ppermute | solution.py:16
  140.1 6.4 %collective-permute-start = (f32[4]{0:T(128)S(1)}, f32[4]{0:T(128)S(1)}, u32[]{:S(2)}, u32[]{:S(2)}) collective-permute-start(f32[4]{0:T(128)S(1)} %add.76), channel_id=1, source_target_pairs={{0,16},{16,32},{32,48},{48,64},{64,80},{80,96},{96,112},{112,128},... | collective-permute-start | bytes 56 | tf_op jit(solution)/shard_map/while/body/eval_jaxpr/ppermute | solution.py:16
  146.7 9.0 %collective-permute-start.1 = (f32[4,128,128]{2,1,0:T(8,128)S(1)}, f32[4,128,128]{2,1,0:T(8,128)S(1)}, u32[]{:S(2)}, u32[]{:S(2)}) collective-permute-start(f32[4,128,128]{2,1,0:T(8,128)S(1)} %multiply_add_fusion.2), channel_id=1, source_target_pairs={{0,16},{16,32},{32,48},{48,64},{64,80},{80,96},{96,112},{112,128},... | collective-permute-start | bytes 786440 | tf_op jit(solution)/shard_map/while/body/eval_jaxpr/ppermute | solution.py:16
  149.2 6.4 %collective-permute-start = (f32[4]{0:T(128)S(1)}, f32[4]{0:T(128)S(1)}, u32[]{:S(2)}, u32[]{:S(2)}) collective-permute-start(f32[4]{0:T(128)S(1)} %add.76), channel_id=1, source_target_pairs={{0,16},{16,32},{32,48},{48,64},{64,80},{80,96},{96,112},{112,128},... | collective-permute-start | bytes 56 | tf_op jit(solution)/shard_map/while/body/eval_jaxpr/ppermute | solution.py:16
  155.8 9.0 %collective-permute-start.1 = (f32[4,128,128]{2,1,0:T(8,128)S(1)}, f32[4,128,128]{2,1,0:T(8,128)S(1)}, u32[]{:S(2)}, u32[]{:S(2)}) collective-permute-start(f32[4,128,128]{2,1,0:T(8,128)S(1)} %multiply_add_fusion.2), channel_id=1, source_target_pairs={{0,16},{16,32},{32,48},{48,64},{64,80},{80,96},{96,112},{112,128},... | collective-permute-start | bytes 786440 | tf_op jit(solution)/shard_map/while/body/eval_jaxpr/ppermute | solution.py:16
  164.9 9.0 %collective-permute-start.1 = (f32[4,128,128]{2,1,0:T(8,128)S(1)}, f32[4,128,128]{2,1,0:T(8,128)S(1)}, u32[]{:S(2)}, u32[]{:S(2)}) collective-permute-start(f32[4,128,128]{2,1,0:T(8,128)S(1)} %multiply_add_fusion.2), channel_id=1, source_target_pairs={{0,16},{16,32},{32,48},{48,64},{64,80},{80,96},{96,112},{112,128},... | collective-permute-start | bytes 786440 | tf_op jit(solution)/shard_map/while/body/eval_jaxpr/ppermute | solution.py:16
  173.9 9.0 %collective-permute-start.1 = (f32[4,128,128]{2,1,0:T(8,128)S(1)}, f32[4,128,128]{2,1,0:T(8,128)S(1)}, u32[]{:S(2)}, u32[]{:S(2)}) collective-permute-start(f32[4,128,128]{2,1,0:T(8,128)S(1)} %multiply_add_fusion.2), channel_id=1, source_target_pairs={{0,16},{16,32},{32,48},{48,64},{64,80},{80,96},{96,112},{112,128},... | collective-permute-start | bytes 786440 | tf_op jit(solution)/shard_map/while/body/eval_jaxpr/ppermute | solution.py:16
  176.5 6.4 %collective-permute-start = (f32[4]{0:T(128)S(1)}, f32[4]{0:T(128)S(1)}, u32[]{:S(2)}, u32[]{:S(2)}) collective-permute-start(f32[4]{0:T(128)S(1)} %add.76), channel_id=1, source_target_pairs={{0,16},{16,32},{32,48},{48,64},{64,80},{80,96},{96,112},{112,128},... | collective-permute-start | bytes 56 | tf_op jit(solution)/shard_map/while/body/eval_jaxpr/ppermute | solution.py:16
  183.0 9.0 %collective-permute-start.1 = (f32[4,128,128]{2,1,0:T(8,128)S(1)}, f32[4,128,128]{2,1,0:T(8,128)S(1)}, u32[]{:S(2)}, u32[]{:S(2)}) collective-permute-start(f32[4,128,128]{2,1,0:T(8,128)S(1)} %multiply_add_fusion.2), channel_id=1, source_target_pairs={{0,16},{16,32},{32,48},{48,64},{64,80},{80,96},{96,112},{112,128},... | collective-permute-start | bytes 786440 | tf_op jit(solution)/shard_map/while/body/eval_jaxpr/ppermute | solution.py:16
  185.6 6.4 %collective-permute-start = (f32[4]{0:T(128)S(1)}, f32[4]{0:T(128)S(1)}, u32[]{:S(2)}, u32[]{:S(2)}) collective-permute-start(f32[4]{0:T(128)S(1)} %add.76), channel_id=1, source_target_pairs={{0,16},{16,32},{32,48},{48,64},{64,80},{80,96},{96,112},{112,128},... | collective-permute-start | bytes 56 | tf_op jit(solution)/shard_map/while/body/eval_jaxpr/ppermute | solution.py:16
  192.1 9.0 %collective-permute-start.1 = (f32[4,128,128]{2,1,0:T(8,128)S(1)}, f32[4,128,128]{2,1,0:T(8,128)S(1)}, u32[]{:S(2)}, u32[]{:S(2)}) collective-permute-start(f32[4,128,128]{2,1,0:T(8,128)S(1)} %multiply_add_fusion.2), channel_id=1, source_target_pairs={{0,16},{16,32},{32,48},{48,64},{64,80},{80,96},{96,112},{112,128},... | collective-permute-start | bytes 786440 | tf_op jit(solution)/shard_map/while/body/eval_jaxpr/ppermute | solution.py:16
  194.7 6.4 %collective-permute-start = (f32[4]{0:T(128)S(1)}, f32[4]{0:T(128)S(1)}, u32[]{:S(2)}, u32[]{:S(2)}) collective-permute-start(f32[4]{0:T(128)S(1)} %add.76), channel_id=1, source_target_pairs={{0,16},{16,32},{32,48},{48,64},{64,80},{80,96},{96,112},{112,128},... | collective-permute-start | bytes 56 | tf_op jit(solution)/shard_map/while/body/eval_jaxpr/ppermute | solution.py:16
  201.2 9.0 %collective-permute-start.1 = (f32[4,128,128]{2,1,0:T(8,128)S(1)}, f32[4,128,128]{2,1,0:T(8,128)S(1)}, u32[]{:S(2)}, u32[]{:S(2)}) collective-permute-start(f32[4,128,128]{2,1,0:T(8,128)S(1)} %multiply_add_fusion.2), channel_id=1, source_target_pairs={{0,16},{16,32},{32,48},{48,64},{64,80},{80,96},{96,112},{112,128},... | collective-permute-start | bytes 786440 | tf_op jit(solution)/shard_map/while/body/eval_jaxpr/ppermute | solution.py:16
  203.8 6.4 %collective-permute-start = (f32[4]{0:T(128)S(1)}, f32[4]{0:T(128)S(1)}, u32[]{:S(2)}, u32[]{:S(2)}) collective-permute-start(f32[4]{0:T(128)S(1)} %add.76), channel_id=1, source_target_pairs={{0,16},{16,32},{32,48},{48,64},{64,80},{80,96},{96,112},{112,128},... | collective-permute-start | bytes 56 | tf_op jit(solution)/shard_map/while/body/eval_jaxpr/ppermute | solution.py:16
  210.3 9.0 %collective-permute-start.1 = (f32[4,128,128]{2,1,0:T(8,128)S(1)}, f32[4,128,128]{2,1,0:T(8,128)S(1)}, u32[]{:S(2)}, u32[]{:S(2)}) collective-permute-start(f32[4,128,128]{2,1,0:T(8,128)S(1)} %multiply_add_fusion.2), channel_id=1, source_target_pairs={{0,16},{16,32},{32,48},{48,64},{64,80},{80,96},{96,112},{112,128},... | collective-permute-start | bytes 786440 | tf_op jit(solution)/shard_map/while/body/eval_jaxpr/ppermute | solution.py:16
  212.9 6.4 %collective-permute-start = (f32[4]{0:T(128)S(1)}, f32[4]{0:T(128)S(1)}, u32[]{:S(2)}, u32[]{:S(2)}) collective-permute-start(f32[4]{0:T(128)S(1)} %add.76), channel_id=1, source_target_pairs={{0,16},{16,32},{32,48},{48,64},{64,80},{80,96},{96,112},{112,128},... | collective-permute-start | bytes 56 | tf_op jit(solution)/shard_map/while/body/eval_jaxpr/ppermute | solution.py:16
  219.4 9.0 %collective-permute-start.1 = (f32[4,128,128]{2,1,0:T(8,128)S(1)}, f32[4,128,128]{2,1,0:T(8,128)S(1)}, u32[]{:S(2)}, u32[]{:S(2)}) collective-permute-start(f32[4,128,128]{2,1,0:T(8,128)S(1)} %multiply_add_fusion.2), channel_id=1, source_target_pairs={{0,16},{16,32},{32,48},{48,64},{64,80},{80,96},{96,112},{112,128},... | collective-permute-start | bytes 786440 | tf_op jit(solution)/shard_map/while/body/eval_jaxpr/ppermute | solution.py:16
  221.9 6.4 %collective-permute-start = (f32[4]{0:T(128)S(1)}, f32[4]{0:T(128)S(1)}, u32[]{:S(2)}, u32[]{:S(2)}) collective-permute-start(f32[4]{0:T(128)S(1)} %add.76), channel_id=1, source_target_pairs={{0,16},{16,32},{32,48},{48,64},{64,80},{80,96},{96,112},{112,128},... | collective-permute-start | bytes 56 | tf_op jit(solution)/shard_map/while/body/eval_jaxpr/ppermute | solution.py:16
  228.5 9.0 %collective-permute-start.1 = (f32[4,128,128]{2,1,0:T(8,128)S(1)}, f32[4,128,128]{2,1,0:T(8,128)S(1)}, u32[]{:S(2)}, u32[]{:S(2)}) collective-permute-start(f32[4,128,128]{2,1,0:T(8,128)S(1)} %multiply_add_fusion.2), channel_id=1, source_target_pairs={{0,16},{16,32},{32,48},{48,64},{64,80},{80,96},{96,112},{112,128},... | collective-permute-start | bytes 786440 | tf_op jit(solution)/shard_map/while/body/eval_jaxpr/ppermute | solution.py:16
  231.0 6.4 %collective-permute-start = (f32[4]{0:T(128)S(1)}, f32[4]{0:T(128)S(1)}, u32[]{:S(2)}, u32[]{:S(2)}) collective-permute-start(f32[4]{0:T(128)S(1)} %add.76), channel_id=1, source_target_pairs={{0,16},{16,32},{32,48},{48,64},{64,80},{80,96},{96,112},{112,128},... | collective-permute-start | bytes 56 | tf_op jit(solution)/shard_map/while/body/eval_jaxpr/ppermute | solution.py:16
  237.6 9.0 %collective-permute-start.1 = (f32[4,128,128]{2,1,0:T(8,128)S(1)}, f32[4,128,128]{2,1,0:T(8,128)S(1)}, u32[]{:S(2)}, u32[]{:S(2)}) collective-permute-start(f32[4,128,128]{2,1,0:T(8,128)S(1)} %multiply_add_fusion.2), channel_id=1, source_target_pairs={{0,16},{16,32},{32,48},{48,64},{64,80},{80,96},{96,112},{112,128},... | collective-permute-start | bytes 786440 | tf_op jit(solution)/shard_map/while/body/eval_jaxpr/ppermute | solution.py:16
  240.1 6.4 %collective-permute-start = (f32[4]{0:T(128)S(1)}, f32[4]{0:T(128)S(1)}, u32[]{:S(2)}, u32[]{:S(2)}) collective-permute-start(f32[4]{0:T(128)S(1)} %add.76), channel_id=1, source_target_pairs={{0,16},{16,32},{32,48},{48,64},{64,80},{80,96},{96,112},{112,128},... | collective-permute-start | bytes 56 | tf_op jit(solution)/shard_map/while/body/eval_jaxpr/ppermute | solution.py:16
  246.7 9.0 %collective-permute-start.1 = (f32[4,128,128]{2,1,0:T(8,128)S(1)}, f32[4,128,128]{2,1,0:T(8,128)S(1)}, u32[]{:S(2)}, u32[]{:S(2)}) collective-permute-start(f32[4,128,128]{2,1,0:T(8,128)S(1)} %multiply_add_fusion.2), channel_id=1, source_target_pairs={{0,16},{16,32},{32,48},{48,64},{64,80},{80,96},{96,112},{112,128},... | collective-permute-start | bytes 786440 | tf_op jit(solution)/shard_map/while/body/eval_jaxpr/ppermute | solution.py:16
  255.8 9.0 %collective-permute-start.1 = (f32[4,128,128]{2,1,0:T(8,128)S(1)}, f32[4,128,128]{2,1,0:T(8,128)S(1)}, u32[]{:S(2)}, u32[]{:S(2)}) collective-permute-start(f32[4,128,128]{2,1,0:T(8,128)S(1)} %multiply_add_fusion.2), channel_id=1, source_target_pairs={{0,16},{16,32},{32,48},{48,64},{64,80},{80,96},{96,112},{112,128},... | collective-permute-start | bytes 786440 | tf_op jit(solution)/shard_map/while/body/eval_jaxpr/ppermute | solution.py:16
  264.9 9.0 %collective-permute-start.1 = (f32[4,128,128]{2,1,0:T(8,128)S(1)}, f32[4,128,128]{2,1,0:T(8,128)S(1)}, u32[]{:S(2)}, u32[]{:S(2)}) collective-permute-start(f32[4,128,128]{2,1,0:T(8,128)S(1)} %multiply_add_fusion.2), channel_id=1, source_target_pairs={{0,16},{16,32},{32,48},{48,64},{64,80},{80,96},{96,112},{112,128},... | collective-permute-start | bytes 786440 | tf_op jit(solution)/shard_map/while/body/eval_jaxpr/ppermute | solution.py:16
  273.9 9.0 %collective-permute-start.1 = (f32[4,128,128]{2,1,0:T(8,128)S(1)}, f32[4,128,128]{2,1,0:T(8,128)S(1)}, u32[]{:S(2)}, u32[]{:S(2)}) collective-permute-start(f32[4,128,128]{2,1,0:T(8,128)S(1)} %multiply_add_fusion.2), channel_id=1, source_target_pairs={{0,16},{16,32},{32,48},{48,64},{64,80},{80,96},{96,112},{112,128},... | collective-permute-start | bytes 786440 | tf_op jit(solution)/shard_map/while/body/eval_jaxpr/ppermute | solution.py:16
  283.0 9.0 %collective-permute-start.1 = (f32[4,128,128]{2,1,0:T(8,128)S(1)}, f32[4,128,128]{2,1,0:T(8,128)S(1)}, u32[]{:S(2)}, u32[]{:S(2)}) collective-permute-start(f32[4,128,128]{2,1,0:T(8,128)S(1)} %multiply_add_fusion.2), channel_id=1, source_target_pairs={{0,16},{16,32},{32,48},{48,64},{64,80},{80,96},{96,112},{112,128},... | collective-permute-start | bytes 786440 | tf_op jit(solution)/shard_map/while/body/eval_jaxpr/ppermute | solution.py:16
  292.1 9.0 %collective-permute-start.1 = (f32[4,128,128]{2,1,0:T(8,128)S(1)}, f32[4,128,128]{2,1,0:T(8,128)S(1)}, u32[]{:S(2)}, u32[]{:S(2)}) collective-permute-start(f32[4,128,128]{2,1,0:T(8,128)S(1)} %multiply_add_fusion.2), channel_id=1, source_target_pairs={{0,16},{16,32},{32,48},{48,64},{64,80},{80,96},{96,112},{112,128},... | collective-permute-start | bytes 786440 | tf_op jit(solution)/shard_map/while/body/eval_jaxpr/ppermute | solution.py:16
  302.0 321.6 %reduce-scatter.4.cloned.1.call-start = ((), (), s32[]{:S(2)}) async-start(), calls=%async_computation.3 | async-start | bytes 3342336
  (21 other events, 1311.3 us)
Sparse Core Ops, SparseCore 0:
  10.1 82.4 all-gather.1
  302.1 225.2 all-reduce.1
  531.6 91.8 reduce-scatter.3
where the time goes:
time: 634 us; the launch traced here: 632 us
  waiting for transfers between devices  299 us (47%)
  starting transfers between devices  260 us (41%)
  blocking collectives  36.8 us (6%)
  between operations  13.9 us (2%)
  local copies, waits for them, and re-layouts  8.45 us (1%)
  matrix products  6.88 us (1%)
    ppermute x62, starting transfers between devices, shifted(): return lax.ppermute(x, axis, pairs)  260 us
    psum x1, waiting for transfers between devices, broadcast(): return lax.psum(jnp.where(mine, x, jnp.zeros_like(x)), axis)  179 us
    unnamed x4, waiting for transfers between devices  95.5 us
    psum x1, blocking collectives, per_device(): squares = lax.psum(jnp.sum(attended * attended, axis=1), 'tp')  36.8 us
    ppermute x62, waiting for transfers between devices, shifted(): return lax.ppermute(x, axis, pairs)  24.8 us
  transfers between devices with their start and end apart: 65, of which 33 were waited for; matrix products, arithmetic and copies ran while one was open for 3% of the time, Pallas kernels for 0%

commit v1 on v0

--- a/solution.py
+++ b/solution.py
@@ -18,7 +18,7 @@
 
 def broadcast(x, axis, root):
     mine = lax.axis_index(axis) == root
-    return lax.psum(jnp.where(mine, x, jnp.zeros_like(x)), axis)
+    return jnp.sum(lax.all_gather(jnp.where(mine, x, jnp.zeros_like(x)), axis), axis=0)
 
 
 def join_states(earlier, later):

time: 634 us -> 499 us (0.79)
  waiting for transfers between devices: 299 us -> 161 us
    psum x1 -> x0, waiting for transfers between devices: 179 us -> none  [broadcast(): return lax.psum(jnp.where(mine, x, jnp.zeros_like(x)), axis)]
    all_gather x0 -> x1, waiting for transfers between devices: none -> 47.4 us  [broadcast(): lax.all_gather(jnp.where(mine, x, jnp.zeros_like(x)), axis)]
    unnamed x4, waiting for transfers between devices: 95.5 us -> 88.7 us
  transfers between devices with their start and end apart: 65 -> 65, of which waited for: 33 -> 33; matrix products, arithmetic and copies ran while one was open for 3% -> 5% of each run, Pallas kernels for 0% -> 0%
where the time goes in v1:
time: 499 us; the launch traced here: 497 us
  starting transfers between devices  260 us (52%)
  waiting for transfers between devices  161 us (32%)
  blocking collectives  36.8 us (7%)
  between operations  13.9 us (3%)
  other arithmetic  9.83 us (2%)
  local copies, waits for them, and re-layouts  7.77 us (2%)
  matrix products  6.92 us (1%)
    ppermute x62, starting transfers between devices, shifted(): return lax.ppermute(x, axis, pairs)  260 us
    unnamed x4, waiting for transfers between devices  88.7 us
    all_gather x1, waiting for transfers between devices, broadcast(): lax.all_gather(jnp.where(mine, x, jnp.zeros_like(x)), axis)  47.4 us
    psum x1, blocking collectives, per_device(): squares = lax.psum(jnp.sum(attended * attended, axis=1), 'tp')  36.8 us
    ppermute x62, waiting for transfers between devices, shifted(): return lax.ppermute(x, axis, pairs)  24.8 us
  transfers between devices with their start and end apart: 65, of which 33 were waited for; matrix products, arithmetic and copies ran while one was open for 5% of the time, Pallas kernels for 0%

profile of v1, /device:TPU:2, one launch (start us, length us, event | category | flops | bytes accessed | tf_op | source)
XLA Modules:
  0.0 496.8 jit_solution(9448950462982039869)
XLA Ops:
  12.8 288.4 %while.13 = (s32[]{:T(128)}, f32[4]{0:T(128)S(1)}, f32[4,128,128]{2,1,0:T(8,128)S(1)}, f32[4]{0:T(128)S(1)}, f32[4,1,1]{0,2,1:T(1,128)S(1)}, /*index=5*/f32[4,128,128]{2,1,0:T(8,128)S(1)}, s32[]{:T(128)}) while((s32[]{:T(128)}, f32[4]{0:T(128)S(1)}, f32[4,128,128]{2,1,0:T(8,128)S(1)}, f32[4]{0:T(128)S(1)}, f32[4,1,1]{0,2,1:T(1,128)S(1)}, ...), condition=%wide.region_3.4_spmd, body=%wide.region_2.3_spmd.sunk | while | flops 131078 | bytes 1835293 | solution.py:75
  14.7 4.1 collective-permute-start
  19.7 2.5 collective-permute-start.1
  22.2 4.4 collective-permute-start
  30.1 4.4 collective-permute-start
  35.4 2.5 collective-permute-start.1
  38.0 4.4 collective-permute-start
  43.3 7.2 %collective-permute-start.1 = (f32[4,128,128]{2,1,0:T(8,128)S(1)}, f32[4,128,128]{2,1,0:T(8,128)S(1)}, u32[]{:S(2)}, u32[]{:S(2)}) collective-permute-start(f32[4,128,128]{2,1,0:T(8,128)S(1)} %multiply_add_fusion.2), channel_id=1, source_target_pairs={{0,16},{16,32},{32,48},{48,64},{64,80},{80,96},{96,112},{112,128},... | collective-permute-start | bytes 786440 | tf_op jit(solution)/shard_map/while/body/eval_jaxpr/ppermute | solution.py:16
  50.6 4.4 collective-permute-start
  55.9 7.1 %collective-permute-start.1 = (f32[4,128,128]{2,1,0:T(8,128)S(1)}, f32[4,128,128]{2,1,0:T(8,128)S(1)}, u32[]{:S(2)}, u32[]{:S(2)}) collective-permute-start(f32[4,128,128]{2,1,0:T(8,128)S(1)} %multiply_add_fusion.2), channel_id=1, source_target_pairs={{0,16},{16,32},{32,48},{48,64},{64,80},{80,96},{96,112},{112,128},... | collective-permute-start | bytes 786440 | tf_op jit(solution)/shard_map/while/body/eval_jaxpr/ppermute | solution.py:16
  63.0 4.5 collective-permute-start
  68.4 7.0 %collective-permute-start.1 = (f32[4,128,128]{2,1,0:T(8,128)S(1)}, f32[4,128,128]{2,1,0:T(8,128)S(1)}, u32[]{:S(2)}, u32[]{:S(2)}) collective-permute-start(f32[4,128,128]{2,1,0:T(8,128)S(1)} %multiply_add_fusion.2), channel_id=1, source_target_pairs={{0,16},{16,32},{32,48},{48,64},{64,80},{80,96},{96,112},{112,128},... | collective-permute-start | bytes 786440 | tf_op jit(solution)/shard_map/while/body/eval_jaxpr/ppermute | solution.py:16
  75.4 4.5 collective-permute-start
  80.8 4.7 collective-permute-start.1
  85.4 4.5 collective-permute-start
  90.8 2.9 collective-permute-start.1
  93.7 4.5 collective-permute-start
  99.1 4.4 collective-permute-start.1
  103.5 5.9 %collective-permute-start = (f32[4]{0:T(128)S(1)}, f32[4]{0:T(128)S(1)}, u32[]{:S(2)}, u32[]{:S(2)}) collective-permute-start(f32[4]{0:T(128)S(1)} %add.74), channel_id=1, source_target_pairs={{0,16},{16,32},{32,48},{48,64},{64,80},{80,96},{96,112},{112,128},... | collective-permute-start | bytes 56 | tf_op jit(solution)/shard_map/while/body/eval_jaxpr/ppermute | solution.py:16
  110.3 2.5 collective-permute-start.1
  112.9 5.6 %collective-permute-start = (f32[4]{0:T(128)S(1)}, f32[4]{0:T(128)S(1)}, u32[]{:S(2)}, u32[]{:S(2)}) collective-permute-start(f32[4]{0:T(128)S(1)} %add.74), channel_id=1, source_target_pairs={{0,16},{16,32},{32,48},{48,64},{64,80},{80,96},{96,112},{112,128},... | collective-permute-start | bytes 56 | tf_op jit(solution)/shard_map/while/body/eval_jaxpr/ppermute | solution.py:16
  119.4 2.5 collective-permute-start.1
  121.9 5.6 %collective-permute-start = (f32[4]{0:T(128)S(1)}, f32[4]{0:T(128)S(1)}, u32[]{:S(2)}, u32[]{:S(2)}) collective-permute-start(f32[4]{0:T(128)S(1)} %add.74), channel_id=1, source_target_pairs={{0,16},{16,32},{32,48},{48,64},{64,80},{80,96},{96,112},{112,128},... | collective-permute-start | bytes 56 | tf_op jit(solution)/shard_map/while/body/eval_jaxpr/ppermute | solution.py:16
  131.0 5.6 %collective-permute-start = (f32[4]{0:T(128)S(1)}, f32[4]{0:T(128)S(1)}, u32[]{:S(2)}, u32[]{:S(2)}) collective-permute-start(f32[4]{0:T(128)S(1)} %add.74), channel_id=1, source_target_pairs={{0,16},{16,32},{32,48},{48,64},{64,80},{80,96},{96,112},{112,128},... | collective-permute-start | bytes 56 | tf_op jit(solution)/shard_map/while/body/eval_jaxpr/ppermute | solution.py:16
  140.1 5.6 %collective-permute-start = (f32[4]{0:T(128)S(1)}, f32[4]{0:T(128)S(1)}, u32[]{:S(2)}, u32[]{:S(2)}) collective-permute-start(f32[4]{0:T(128)S(1)} %add.74), channel_id=1, source_target_pairs={{0,16},{16,32},{32,48},{48,64},{64,80},{80,96},{96,112},{112,128},... | collective-permute-start | bytes 56 | tf_op jit(solution)/shard_map/while/body/eval_jaxpr/ppermute | solution.py:16
  149.2 5.6 %collective-permute-start = (f32[4]{0:T(128)S(1)}, f32[4]{0:T(128)S(1)}, u32[]{:S(2)}, u32[]{:S(2)}) collective-permute-start(f32[4]{0:T(128)S(1)} %add.74), channel_id=1, source_target_pairs={{0,16},{16,32},{32,48},{48,64},{64,80},{80,96},{96,112},{112,128},... | collective-permute-start | bytes 56 | tf_op jit(solution)/shard_map/while/body/eval_jaxpr/ppermute | solution.py:16
  158.3 5.6 %collective-permute-start = (f32[4]{0:T(128)S(1)}, f32[4]{0:T(128)S(1)}, u32[]{:S(2)}, u32[]{:S(2)}) collective-permute-start(f32[4]{0:T(128)S(1)} %add.74), channel_id=1, source_target_pairs={{0,16},{16,32},{32,48},{48,64},{64,80},{80,96},{96,112},{112,128},... | collective-permute-start | bytes 56 | tf_op jit(solution)/shard_map/while/body/eval_jaxpr/ppermute | solution.py:16
  167.4 5.6 %collective-permute-start = (f32[4]{0:T(128)S(1)}, f32[4]{0:T(128)S(1)}, u32[]{:S(2)}, u32[]{:S(2)}) collective-permute-start(f32[4]{0:T(128)S(1)} %add.74), channel_id=1, source_target_pairs={{0,16},{16,32},{32,48},{48,64},{64,80},{80,96},{96,112},{112,128},... | collective-permute-start | bytes 56 | tf_op jit(solution)/shard_map/while/body/eval_jaxpr/ppermute | solution.py:16
  176.5 5.6 %collective-permute-start = (f32[4]{0:T(128)S(1)}, f32[4]{0:T(128)S(1)}, u32[]{:S(2)}, u32[]{:S(2)}) collective-permute-start(f32[4]{0:T(128)S(1)} %add.74), channel_id=1, source_target_pairs={{0,16},{16,32},{32,48},{48,64},{64,80},{80,96},{96,112},{112,128},... | collective-permute-start | bytes 56 | tf_op jit(solution)/shard_map/while/body/eval_jaxpr/ppermute | solution.py:16
  185.6 5.6 %collective-permute-start = (f32[4]{0:T(128)S(1)}, f32[4]{0:T(128)S(1)}, u32[]{:S(2)}, u32[]{:S(2)}) collective-permute-start(f32[4]{0:T(128)S(1)} %add.74), channel_id=1, source_target_pairs={{0,16},{16,32},{32,48},{48,64},{64,80},{80,96},{96,112},{112,128},... | collective-permute-start | bytes 56 | tf_op jit(solution)/shard_map/while/body/eval_jaxpr/ppermute | solution.py:16
  194.7 5.6 %collective-permute-start = (f32[4]{0:T(128)S(1)}, f32[4]{0:T(128)S(1)}, u32[]{:S(2)}, u32[]{:S(2)}) collective-permute-start(f32[4]{0:T(128)S(1)} %add.74), channel_id=1, source_target_pairs={{0,16},{16,32},{32,48},{48,64},{64,80},{80,96},{96,112},{112,128},... | collective-permute-start | bytes 56 | tf_op jit(solution)/shard_map/while/body/eval_jaxpr/ppermute | solution.py:16
  203.8 5.6 %collective-permute-start = (f32[4]{0:T(128)S(1)}, f32[4]{0:T(128)S(1)}, u32[]{:S(2)}, u32[]{:S(2)}) collective-permute-start(f32[4]{0:T(128)S(1)} %add.74), channel_id=1, source_target_pairs={{0,16},{16,32},{32,48},{48,64},{64,80},{80,96},{96,112},{112,128},... | collective-permute-start | bytes 56 | tf_op jit(solution)/shard_map/while/body/eval_jaxpr/ppermute | solution.py:16
  212.9 5.6 %collective-permute-start = (f32[4]{0:T(128)S(1)}, f32[4]{0:T(128)S(1)}, u32[]{:S(2)}, u32[]{:S(2)}) collective-permute-start(f32[4]{0:T(128)S(1)} %add.74), channel_id=1, source_target_pairs={{0,16},{16,32},{32,48},{48,64},{64,80},{80,96},{96,112},{112,128},... | collective-permute-start | bytes 56 | tf_op jit(solution)/shard_map/while/body/eval_jaxpr/ppermute | solution.py:16
  221.9 5.6 %collective-permute-start = (f32[4]{0:T(128)S(1)}, f32[4]{0:T(128)S(1)}, u32[]{:S(2)}, u32[]{:S(2)}) collective-permute-start(f32[4]{0:T(128)S(1)} %add.74), channel_id=1, source_target_pairs={{0,16},{16,32},{32,48},{48,64},{64,80},{80,96},{96,112},{112,128},... | collective-permute-start | bytes 56 | tf_op jit(solution)/shard_map/while/body/eval_jaxpr/ppermute | solution.py:16
  231.0 5.6 %collective-permute-start = (f32[4]{0:T(128)S(1)}, f32[4]{0:T(128)S(1)}, u32[]{:S(2)}, u32[]{:S(2)}) collective-permute-start(f32[4]{0:T(128)S(1)} %add.74), channel_id=1, source_target_pairs={{0,16},{16,32},{32,48},{48,64},{64,80},{80,96},{96,112},{112,128},... | collective-permute-start | bytes 56 | tf_op jit(solution)/shard_map/while/body/eval_jaxpr/ppermute | solution.py:16
  240.1 5.6 %collective-permute-start = (f32[4]{0:T(128)S(1)}, f32[4]{0:T(128)S(1)}, u32[]{:S(2)}, u32[]{:S(2)}) collective-permute-start(f32[4]{0:T(128)S(1)} %add.74), channel_id=1, source_target_pairs={{0,16},{16,32},{32,48},{48,64},{64,80},{80,96},{96,112},{112,128},... | collective-permute-start | bytes 56 | tf_op jit(solution)/shard_map/while/body/eval_jaxpr/ppermute | solution.py:16
  249.2 5.6 %collective-permute-start = (f32[4]{0:T(128)S(1)}, f32[4]{0:T(128)S(1)}, u32[]{:S(2)}, u32[]{:S(2)}) collective-permute-start(f32[4]{0:T(128)S(1)} %add.74), channel_id=1, source_target_pairs={{0,16},{16,32},{32,48},{48,64},{64,80},{80,96},{96,112},{112,128},... | collective-permute-start | bytes 56 | tf_op jit(solution)/shard_map/while/body/eval_jaxpr/ppermute | solution.py:16
  258.3 5.6 %collective-permute-start = (f32[4]{0:T(128)S(1)}, f32[4]{0:T(128)S(1)}, u32[]{:S(2)}, u32[]{:S(2)}) collective-permute-start(f32[4]{0:T(128)S(1)} %add.74), channel_id=1, source_target_pairs={{0,16},{16,32},{32,48},{48,64},{64,80},{80,96},{96,112},{112,128},... | collective-permute-start | bytes 56 | tf_op jit(solution)/shard_map/while/body/eval_jaxpr/ppermute | solution.py:16
  267.4 5.6 %collective-permute-start = (f32[4]{0:T(128)S(1)}, f32[4]{0:T(128)S(1)}, u32[]{:S(2)}, u32[]{:S(2)}) collective-permute-start(f32[4]{0:T(128)S(1)} %add.74), channel_id=1, source_target_pairs={{0,16},{16,32},{32,48},{48,64},{64,80},{80,96},{96,112},{112,128},... | collective-permute-start | bytes 56 | tf_op jit(solution)/shard_map/while/body/eval_jaxpr/ppermute | solution.py:16
  276.5 5.6 %collective-permute-start = (f32[4]{0:T(128)S(1)}, f32[4]{0:T(128)S(1)}, u32[]{:S(2)}, u32[]{:S(2)}) collective-permute-start(f32[4]{0:T(128)S(1)} %add.74), channel_id=1, source_target_pairs={{0,16},{16,32},{32,48},{48,64},{64,80},{80,96},{96,112},{112,128},... | collective-permute-start | bytes 56 | tf_op jit(solution)/shard_map/while/body/eval_jaxpr/ppermute | solution.py:16
  285.6 5.6 %collective-permute-start = (f32[4]{0:T(128)S(1)}, f32[4]{0:T(128)S(1)}, u32[]{:S(2)}, u32[]{:S(2)}) collective-permute-start(f32[4]{0:T(128)S(1)} %add.74), channel_id=1, source_target_pairs={{0,16},{16,32},{32,48},{48,64},{64,80},{80,96},{96,112},{112,128},... | collective-permute-start | bytes 56 | tf_op jit(solution)/shard_map/while/body/eval_jaxpr/ppermute | solution.py:16
  294.7 5.6 %collective-permute-start = (f32[4]{0:T(128)S(1)}, f32[4]{0:T(128)S(1)}, u32[]{:S(2)}, u32[]{:S(2)}) collective-permute-start(f32[4]{0:T(128)S(1)} %add.74), channel_id=1, source_target_pairs={{0,16},{16,32},{32,48},{48,64},{64,80},{80,96},{96,112},{112,128},... | collective-permute-start | bytes 56 | tf_op jit(solution)/shard_map/while/body/eval_jaxpr/ppermute | solution.py:16
  303.5 36.8 %psum.7 = f32[256]{0:T(256)S(1)} all-reduce(f32[256]{0:T(256)S(1)} %get-tuple-element.79), channel_id=1, replica_groups=mesh['ctx'=32,'tp'=16] {'tp'}, use_global_device_ids=true, to_apply=%region_5.6 | all-reduce | flops 256 | bytes 2048 | tf_op jit(solution)/shard_map/psum | solution.py:87
  341.1 4.8 convolution_convert_fusion
  345.9 2.8 copy.38
  348.7 47.4 %all-gather.6.cloned.1.call-done = f32[128,128,128]{2,1,0:T(8,128)} async-done(((f32[4,128,128]{2,1,0:T(8,128)}), f32[128,128,128]{2,1,0:T(8,128)}) %all-gather.6.cloned.1.call-update) | async-done | bytes 8388624 | tf_op jit(solution)/shard_map/all_gather | solution.py:21
  396.1 3.8 reduce_sum.19
  400.6 88.0 %reduce-scatter.4.cloned.1.call-done = bf16[384,256]{1,0:T(8,128)(2,1)} async-done(((bf16[6144,256]{1,0:T(8,128)(2,1)}), bf16[384,256]{1,0:T(8,128)(2,1)}) %reduce-scatter.4.cloned.1.call-update) | async-done | bytes 196624
  (190 shorter events, 91.1 us)
Async XLA Ops:
  7.2 333.9 %all-gather.4.cloned.1.call-start = ((), (), s32[]{:S(2)}) async-start(), calls=%async_computation.1 | async-start | bytes 6488064 | tf_op jit(solution)/shard_map/all_gather | solution.py:92
  7.9 388.2 %all-gather.6.cloned.1.call-start = ((), (), s32[]{:S(2)}) async-start(), calls=%async_computation.2 | async-start | bytes 8650752 | tf_op jit(solution)/shard_map/all_gather | solution.py:21
  12.9 6.7 %collective-permute-start.1 = (f32[4,128,128]{2,1,0:T(8,128)S(1)}, f32[4,128,128]{2,1,0:T(8,128)S(1)}, u32[]{:S(2)}, u32[]{:S(2)}) collective-permute-start(f32[4,128,128]{2,1,0:T(8,128)S(1)} %multiply_add_fusion.2), channel_id=1, source_target_pairs={{0,16},{16,32},{32,48},{48,64},{64,80},{80,96},{96,112},{112,128},... | collective-permute-start | bytes 786440 | tf_op jit(solution)/shard_map/while/body/eval_jaxpr/ppermute | solution.py:16
  19.7 7.8 %collective-permute-start.1 = (f32[4,128,128]{2,1,0:T(8,128)S(1)}, f32[4,128,128]{2,1,0:T(8,128)S(1)}, u32[]{:S(2)}, u32[]{:S(2)}) collective-permute-start(f32[4,128,128]{2,1,0:T(8,128)S(1)} %multiply_add_fusion.2), channel_id=1, source_target_pairs={{0,16},{16,32},{32,48},{48,64},{64,80},{80,96},{96,112},{112,128},... | collective-permute-start | bytes 786440 | tf_op jit(solution)/shard_map/while/body/eval_jaxpr/ppermute | solution.py:16
  27.5 7.8 %collective-permute-start.1 = (f32[4,128,128]{2,1,0:T(8,128)S(1)}, f32[4,128,128]{2,1,0:T(8,128)S(1)}, u32[]{:S(2)}, u32[]{:S(2)}) collective-permute-start(f32[4,128,128]{2,1,0:T(8,128)S(1)} %multiply_add_fusion.2), channel_id=1, source_target_pairs={{0,16},{16,32},{32,48},{48,64},{64,80},{80,96},{96,112},{112,128},... | collective-permute-start | bytes 786440 | tf_op jit(solution)/shard_map/while/body/eval_jaxpr/ppermute | solution.py:16
  35.4 7.8 %collective-permute-start.1 = (f32[4,128,128]{2,1,0:T(8,128)S(1)}, f32[4,128,128]{2,1,0:T(8,128)S(1)}, u32[]{:S(2)}, u32[]{:S(2)}) collective-permute-start(f32[4,128,128]{2,1,0:T(8,128)S(1)} %multiply_add_fusion.2), channel_id=1, source_target_pairs={{0,16},{16,32},{32,48},{48,64},{64,80},{80,96},{96,112},{112,128},... | collective-permute-start | bytes 786440 | tf_op jit(solution)/shard_map/while/body/eval_jaxpr/ppermute | solution.py:16
  43.3 12.5 %collective-permute-start.1 = (f32[4,128,128]{2,1,0:T(8,128)S(1)}, f32[4,128,128]{2,1,0:T(8,128)S(1)}, u32[]{:S(2)}, u32[]{:S(2)}) collective-permute-start(f32[4,128,128]{2,1,0:T(8,128)S(1)} %multiply_add_fusion.2), channel_id=1, source_target_pairs={{0,16},{16,32},{32,48},{48,64},{64,80},{80,96},{96,112},{112,128},... | collective-permute-start | bytes 786440 | tf_op jit(solution)/shard_map/while/body/eval_jaxpr/ppermute | solution.py:16
  55.9 12.4 %collective-permute-start.1 = (f32[4,128,128]{2,1,0:T(8,128)S(1)}, f32[4,128,128]{2,1,0:T(8,128)S(1)}, u32[]{:S(2)}, u32[]{:S(2)}) collective-permute-start(f32[4,128,128]{2,1,0:T(8,128)S(1)} %multiply_add_fusion.2), channel_id=1, source_target_pairs={{0,16},{16,32},{32,48},{48,64},{64,80},{80,96},{96,112},{112,128},... | collective-permute-start | bytes 786440 | tf_op jit(solution)/shard_map/while/body/eval_jaxpr/ppermute | solution.py:16
  68.4 12.3 %collective-permute-start.1 = (f32[4,128,128]{2,1,0:T(8,128)S(1)}, f32[4,128,128]{2,1,0:T(8,128)S(1)}, u32[]{:S(2)}, u32[]{:S(2)}) collective-permute-start(f32[4,128,128]{2,1,0:T(8,128)S(1)} %multiply_add_fusion.2), channel_id=1, source_target_pairs={{0,16},{16,32},{32,48},{48,64},{64,80},{80,96},{96,112},{112,128},... | collective-permute-start | bytes 786440 | tf_op jit(solution)/shard_map/while/body/eval_jaxpr/ppermute | solution.py:16
  80.8 10.0 %collective-permute-start.1 = (f32[4,128,128]{2,1,0:T(8,128)S(1)}, f32[4,128,128]{2,1,0:T(8,128)S(1)}, u32[]{:S(2)}, u32[]{:S(2)}) collective-permute-start(f32[4,128,128]{2,1,0:T(8,128)S(1)} %multiply_add_fusion.2), channel_id=1, source_target_pairs={{0,16},{16,32},{32,48},{48,64},{64,80},{80,96},{96,112},{112,128},... | collective-permute-start | bytes 786440 | tf_op jit(solution)/shard_map/while/body/eval_jaxpr/ppermute | solution.py:16
  90.8 8.2 %collective-permute-start.1 = (f32[4,128,128]{2,1,0:T(8,128)S(1)}, f32[4,128,128]{2,1,0:T(8,128)S(1)}, u32[]{:S(2)}, u32[]{:S(2)}) collective-permute-start(f32[4,128,128]{2,1,0:T(8,128)S(1)} %multiply_add_fusion.2), channel_id=1, source_target_pairs={{0,16},{16,32},{32,48},{48,64},{64,80},{80,96},{96,112},{112,128},... | collective-permute-start | bytes 786440 | tf_op jit(solution)/shard_map/while/body/eval_jaxpr/ppermute | solution.py:16
  99.1 11.1 %collective-permute-start.1 = (f32[4,128,128]{2,1,0:T(8,128)S(1)}, f32[4,128,128]{2,1,0:T(8,128)S(1)}, u32[]{:S(2)}, u32[]{:S(2)}) collective-permute-start(f32[4,128,128]{2,1,0:T(8,128)S(1)} %multiply_add_fusion.2), channel_id=1, source_target_pairs={{0,16},{16,32},{32,48},{48,64},{64,80},{80,96},{96,112},{112,128},... | collective-permute-start | bytes 786440 | tf_op jit(solution)/shard_map/while/body/eval_jaxpr/ppermute | solution.py:16
  103.5 6.7 %collective-permute-start = (f32[4]{0:T(128)S(1)}, f32[4]{0:T(128)S(1)}, u32[]{:S(2)}, u32[]{:S(2)}) collective-permute-start(f32[4]{0:T(128)S(1)} %add.74), channel_id=1, source_target_pairs={{0,16},{16,32},{32,48},{48,64},{64,80},{80,96},{96,112},{112,128},... | collective-permute-start | bytes 56 | tf_op jit(solution)/shard_map/while/body/eval_jaxpr/ppermute | solution.py:16
  110.3 9.0 %collective-permute-start.1 = (f32[4,128,128]{2,1,0:T(8,128)S(1)}, f32[4,128,128]{2,1,0:T(8,128)S(1)}, u32[]{:S(2)}, u32[]{:S(2)}) collective-permute-start(f32[4,128,128]{2,1,0:T(8,128)S(1)} %multiply_add_fusion.2), channel_id=1, source_target_pairs={{0,16},{16,32},{32,48},{48,64},{64,80},{80,96},{96,112},{112,128},... | collective-permute-start | bytes 786440 | tf_op jit(solution)/shard_map/while/body/eval_jaxpr/ppermute | solution.py:16
  112.9 6.4 %collective-permute-start = (f32[4]{0:T(128)S(1)}, f32[4]{0:T(128)S(1)}, u32[]{:S(2)}, u32[]{:S(2)}) collective-permute-start(f32[4]{0:T(128)S(1)} %add.74), channel_id=1, source_target_pairs={{0,16},{16,32},{32,48},{48,64},{64,80},{80,96},{96,112},{112,128},... | collective-permute-start | bytes 56 | tf_op jit(solution)/shard_map/while/body/eval_jaxpr/ppermute | solution.py:16
  119.4 9.0 %collective-permute-start.1 = (f32[4,128,128]{2,1,0:T(8,128)S(1)}, f32[4,128,128]{2,1,0:T(8,128)S(1)}, u32[]{:S(2)}, u32[]{:S(2)}) collective-permute-start(f32[4,128,128]{2,1,0:T(8,128)S(1)} %multiply_add_fusion.2), channel_id=1, source_target_pairs={{0,16},{16,32},{32,48},{48,64},{64,80},{80,96},{96,112},{112,128},... | collective-permute-start | bytes 786440 | tf_op jit(solution)/shard_map/while/body/eval_jaxpr/ppermute | solution.py:16
  121.9 6.4 %collective-permute-start = (f32[4]{0:T(128)S(1)}, f32[4]{0:T(128)S(1)}, u32[]{:S(2)}, u32[]{:S(2)}) collective-permute-start(f32[4]{0:T(128)S(1)} %add.74), channel_id=1, source_target_pairs={{0,16},{16,32},{32,48},{48,64},{64,80},{80,96},{96,112},{112,128},... | collective-permute-start | bytes 56 | tf_op jit(solution)/shard_map/while/body/eval_jaxpr/ppermute | solution.py:16
  128.5 9.0 %collective-permute-start.1 = (f32[4,128,128]{2,1,0:T(8,128)S(1)}, f32[4,128,128]{2,1,0:T(8,128)S(1)}, u32[]{:S(2)}, u32[]{:S(2)}) collective-permute-start(f32[4,128,128]{2,1,0:T(8,128)S(1)} %multiply_add_fusion.2), channel_id=1, source_target_pairs={{0,16},{16,32},{32,48},{48,64},{64,80},{80,96},{96,112},{112,128},... | collective-permute-start | bytes 786440 | tf_op jit(solution)/shard_map/while/body/eval_jaxpr/ppermute | solution.py:16
  131.0 6.4 %collective-permute-start = (f32[4]{0:T(128)S(1)}, f32[4]{0:T(128)S(1)}, u32[]{:S(2)}, u32[]{:S(2)}) collective-permute-start(f32[4]{0:T(128)S(1)} %add.74), channel_id=1, source_target_pairs={{0,16},{16,32},{32,48},{48,64},{64,80},{80,96},{96,112},{112,128},... | collective-permute-start | bytes 56 | tf_op jit(solution)/shard_map/while/body/eval_jaxpr/ppermute | solution.py:16
  137.6 9.0 %collective-permute-start.1 = (f32[4,128,128]{2,1,0:T(8,128)S(1)}, f32[4,128,128]{2,1,0:T(8,128)S(1)}, u32[]{:S(2)}, u32[]{:S(2)}) collective-permute-start(f32[4,128,128]{2,1,0:T(8,128)S(1)} %multiply_add_fusion.2), channel_id=1, source_target_pairs={{0,16},{16,32},{32,48},{48,64},{64,80},{80,96},{96,112},{112,128},... | collective-permute-start | bytes 786440 | tf_op jit(solution)/shard_map/while/body/eval_jaxpr/ppermute | solution.py:16
  140.1 6.4 %collective-permute-start = (f32[4]{0:T(128)S(1)}, f32[4]{0:T(128)S(1)}, u32[]{:S(2)}, u32[]{:S(2)}) collective-permute-start(f32[4]{0:T(128)S(1)} %add.74), channel_id=1, source_target_pairs={{0,16},{16,32},{32,48},{48,64},{64,80},{80,96},{96,112},{112,128},... | collective-permute-start | bytes 56 | tf_op jit(solution)/shard_map/while/body/eval_jaxpr/ppermute | solution.py:16
  146.7 9.0 %collective-permute-start.1 = (f32[4,128,128]{2,1,0:T(8,128)S(1)}, f32[4,128,128]{2,1,0:T(8,128)S(1)}, u32[]{:S(2)}, u32[]{:S(2)}) collective-permute-start(f32[4,128,128]{2,1,0:T(8,128)S(1)} %multiply_add_fusion.2), channel_id=1, source_target_pairs={{0,16},{16,32},{32,48},{48,64},{64,80},{80,96},{96,112},{112,128},... | collective-permute-start | bytes 786440 | tf_op jit(solution)/shard_map/while/body/eval_jaxpr/ppermute | solution.py:16
  149.2 6.4 %collective-permute-start = (f32[4]{0:T(128)S(1)}, f32[4]{0:T(128)S(1)}, u32[]{:S(2)}, u32[]{:S(2)}) collective-permute-start(f32[4]{0:T(128)S(1)} %add.74), channel_id=1, source_target_pairs={{0,16},{16,32},{32,48},{48,64},{64,80},{80,96},{96,112},{112,128},... | collective-permute-start | bytes 56 | tf_op jit(solution)/shard_map/while/body/eval_jaxpr/ppermute | solution.py:16
  155.8 9.0 %collective-permute-start.1 = (f32[4,128,128]{2,1,0:T(8,128)S(1)}, f32[4,128,128]{2,1,0:T(8,128)S(1)}, u32[]{:S(2)}, u32[]{:S(2)}) collective-permute-start(f32[4,128,128]{2,1,0:T(8,128)S(1)} %multiply_add_fusion.2), channel_id=1, source_target_pairs={{0,16},{16,32},{32,48},{48,64},{64,80},{80,96},{96,112},{112,128},... | collective-permute-start | bytes 786440 | tf_op jit(solution)/shard_map/while/body/eval_jaxpr/ppermute | solution.py:16
  164.9 9.0 %collective-permute-start.1 = (f32[4,128,128]{2,1,0:T(8,128)S(1)}, f32[4,128,128]{2,1,0:T(8,128)S(1)}, u32[]{:S(2)}, u32[]{:S(2)}) collective-permute-start(f32[4,128,128]{2,1,0:T(8,128)S(1)} %multiply_add_fusion.2), channel_id=1, source_target_pairs={{0,16},{16,32},{32,48},{48,64},{64,80},{80,96},{96,112},{112,128},... | collective-permute-start | bytes 786440 | tf_op jit(solution)/shard_map/while/body/eval_jaxpr/ppermute | solution.py:16
  173.9 9.0 %collective-permute-start.1 = (f32[4,128,128]{2,1,0:T(8,128)S(1)}, f32[4,128,128]{2,1,0:T(8,128)S(1)}, u32[]{:S(2)}, u32[]{:S(2)}) collective-permute-start(f32[4,128,128]{2,1,0:T(8,128)S(1)} %multiply_add_fusion.2), channel_id=1, source_target_pairs={{0,16},{16,32},{32,48},{48,64},{64,80},{80,96},{96,112},{112,128},... | collective-permute-start | bytes 786440 | tf_op jit(solution)/shard_map/while/body/eval_jaxpr/ppermute | solution.py:16
  176.5 6.4 %collective-permute-start = (f32[4]{0:T(128)S(1)}, f32[4]{0:T(128)S(1)}, u32[]{:S(2)}, u32[]{:S(2)}) collective-permute-start(f32[4]{0:T(128)S(1)} %add.74), channel_id=1, source_target_pairs={{0,16},{16,32},{32,48},{48,64},{64,80},{80,96},{96,112},{112,128},... | collective-permute-start | bytes 56 | tf_op jit(solution)/shard_map/while/body/eval_jaxpr/ppermute | solution.py:16
  183.0 9.0 %collective-permute-start.1 = (f32[4,128,128]{2,1,0:T(8,128)S(1)}, f32[4,128,128]{2,1,0:T(8,128)S(1)}, u32[]{:S(2)}, u32[]{:S(2)}) collective-permute-start(f32[4,128,128]{2,1,0:T(8,128)S(1)} %multiply_add_fusion.2), channel_id=1, source_target_pairs={{0,16},{16,32},{32,48},{48,64},{64,80},{80,96},{96,112},{112,128},... | collective-permute-start | bytes 786440 | tf_op jit(solution)/shard_map/while/body/eval_jaxpr/ppermute | solution.py:16
  185.6 6.4 %collective-permute-start = (f32[4]{0:T(128)S(1)}, f32[4]{0:T(128)S(1)}, u32[]{:S(2)}, u32[]{:S(2)}) collective-permute-start(f32[4]{0:T(128)S(1)} %add.74), channel_id=1, source_target_pairs={{0,16},{16,32},{32,48},{48,64},{64,80},{80,96},{96,112},{112,128},... | collective-permute-start | bytes 56 | tf_op jit(solution)/shard_map/while/body/eval_jaxpr/ppermute | solution.py:16
  192.1 9.0 %collective-permute-start.1 = (f32[4,128,128]{2,1,0:T(8,128)S(1)}, f32[4,128,128]{2,1,0:T(8,128)S(1)}, u32[]{:S(2)}, u32[]{:S(2)}) collective-permute-start(f32[4,128,128]{2,1,0:T(8,128)S(1)} %multiply_add_fusion.2), channel_id=1, source_target_pairs={{0,16},{16,32},{32,48},{48,64},{64,80},{80,96},{96,112},{112,128},... | collective-permute-start | bytes 786440 | tf_op jit(solution)/shard_map/while/body/eval_jaxpr/ppermute | solution.py:16
  194.7 6.4 %collective-permute-start = (f32[4]{0:T(128)S(1)}, f32[4]{0:T(128)S(1)}, u32[]{:S(2)}, u32[]{:S(2)}) collective-permute-start(f32[4]{0:T(128)S(1)} %add.74), channel_id=1, source_target_pairs={{0,16},{16,32},{32,48},{48,64},{64,80},{80,96},{96,112},{112,128},... | collective-permute-start | bytes 56 | tf_op jit(solution)/shard_map/while/body/eval_jaxpr/ppermute | solution.py:16
  201.2 9.0 %collective-permute-start.1 = (f32[4,128,128]{2,1,0:T(8,128)S(1)}, f32[4,128,128]{2,1,0:T(8,128)S(1)}, u32[]{:S(2)}, u32[]{:S(2)}) collective-permute-start(f32[4,128,128]{2,1,0:T(8,128)S(1)} %multiply_add_fusion.2), channel_id=1, source_target_pairs={{0,16},{16,32},{32,48},{48,64},{64,80},{80,96},{96,112},{112,128},... | collective-permute-start | bytes 786440 | tf_op jit(solution)/shard_map/while/body/eval_jaxpr/ppermute | solution.py:16
  203.8 6.4 %collective-permute-start = (f32[4]{0:T(128)S(1)}, f32[4]{0:T(128)S(1)}, u32[]{:S(2)}, u32[]{:S(2)}) collective-permute-start(f32[4]{0:T(128)S(1)} %add.74), channel_id=1, source_target_pairs={{0,16},{16,32},{32,48},{48,64},{64,80},{80,96},{96,112},{112,128},... | collective-permute-start | bytes 56 | tf_op jit(solution)/shard_map/while/body/eval_jaxpr/ppermute | solution.py:16
  210.3 9.0 %collective-permute-start.1 = (f32[4,128,128]{2,1,0:T(8,128)S(1)}, f32[4,128,128]{2,1,0:T(8,128)S(1)}, u32[]{:S(2)}, u32[]{:S(2)}) collective-permute-start(f32[4,128,128]{2,1,0:T(8,128)S(1)} %multiply_add_fusion.2), channel_id=1, source_target_pairs={{0,16},{16,32},{32,48},{48,64},{64,80},{80,96},{96,112},{112,128},... | collective-permute-start | bytes 786440 | tf_op jit(solution)/shard_map/while/body/eval_jaxpr/ppermute | solution.py:16
  212.9 6.4 %collective-permute-start = (f32[4]{0:T(128)S(1)}, f32[4]{0:T(128)S(1)}, u32[]{:S(2)}, u32[]{:S(2)}) collective-permute-start(f32[4]{0:T(128)S(1)} %add.74), channel_id=1, source_target_pairs={{0,16},{16,32},{32,48},{48,64},{64,80},{80,96},{96,112},{112,128},... | collective-permute-start | bytes 56 | tf_op jit(solution)/shard_map/while/body/eval_jaxpr/ppermute | solution.py:16
  219.4 9.0 %collective-permute-start.1 = (f32[4,128,128]{2,1,0:T(8,128)S(1)}, f32[4,128,128]{2,1,0:T(8,128)S(1)}, u32[]{:S(2)}, u32[]{:S(2)}) collective-permute-start(f32[4,128,128]{2,1,0:T(8,128)S(1)} %multiply_add_fusion.2), channel_id=1, source_target_pairs={{0,16},{16,32},{32,48},{48,64},{64,80},{80,96},{96,112},{112,128},... | collective-permute-start | bytes 786440 | tf_op jit(solution)/shard_map/while/body/eval_jaxpr/ppermute | solution.py:16
  221.9 6.4 %collective-permute-start = (f32[4]{0:T(128)S(1)}, f32[4]{0:T(128)S(1)}, u32[]{:S(2)}, u32[]{:S(2)}) collective-permute-start(f32[4]{0:T(128)S(1)} %add.74), channel_id=1, source_target_pairs={{0,16},{16,32},{32,48},{48,64},{64,80},{80,96},{96,112},{112,128},... | collective-permute-start | bytes 56 | tf_op jit(solution)/shard_map/while/body/eval_jaxpr/ppermute | solution.py:16
  228.5 9.0 %collective-permute-start.1 = (f32[4,128,128]{2,1,0:T(8,128)S(1)}, f32[4,128,128]{2,1,0:T(8,128)S(1)}, u32[]{:S(2)}, u32[]{:S(2)}) collective-permute-start(f32[4,128,128]{2,1,0:T(8,128)S(1)} %multiply_add_fusion.2), channel_id=1, source_target_pairs={{0,16},{16,32},{32,48},{48,64},{64,80},{80,96},{96,112},{112,128},... | collective-permute-start | bytes 786440 | tf_op jit(solution)/shard_map/while/body/eval_jaxpr/ppermute | solution.py:16
  231.0 6.4 %collective-permute-start = (f32[4]{0:T(128)S(1)}, f32[4]{0:T(128)S(1)}, u32[]{:S(2)}, u32[]{:S(2)}) collective-permute-start(f32[4]{0:T(128)S(1)} %add.74), channel_id=1, source_target_pairs={{0,16},{16,32},{32,48},{48,64},{64,80},{80,96},{96,112},{112,128},... | collective-permute-start | bytes 56 | tf_op jit(solution)/shard_map/while/body/eval_jaxpr/ppermute | solution.py:16
  237.6 9.0 %collective-permute-start.1 = (f32[4,128,128]{2,1,0:T(8,128)S(1)}, f32[4,128,128]{2,1,0:T(8,128)S(1)}, u32[]{:S(2)}, u32[]{:S(2)}) collective-permute-start(f32[4,128,128]{2,1,0:T(8,128)S(1)} %multiply_add_fusion.2), channel_id=1, source_target_pairs={{0,16},{16,32},{32,48},{48,64},{64,80},{80,96},{96,112},{112,128},... | collective-permute-start | bytes 786440 | tf_op jit(solution)/shard_map/while/body/eval_jaxpr/ppermute | solution.py:16
  240.1 6.4 %collective-permute-start = (f32[4]{0:T(128)S(1)}, f32[4]{0:T(128)S(1)}, u32[]{:S(2)}, u32[]{:S(2)}) collective-permute-start(f32[4]{0:T(128)S(1)} %add.74), channel_id=1, source_target_pairs={{0,16},{16,32},{32,48},{48,64},{64,80},{80,96},{96,112},{112,128},... | collective-permute-start | bytes 56 | tf_op jit(solution)/shard_map/while/body/eval_jaxpr/ppermute | solution.py:16
  246.7 9.0 %collective-permute-start.1 = (f32[4,128,128]{2,1,0:T(8,128)S(1)}, f32[4,128,128]{2,1,0:T(8,128)S(1)}, u32[]{:S(2)}, u32[]{:S(2)}) collective-permute-start(f32[4,128,128]{2,1,0:T(8,128)S(1)} %multiply_add_fusion.2), channel_id=1, source_target_pairs={{0,16},{16,32},{32,48},{48,64},{64,80},{80,96},{96,112},{112,128},... | collective-permute-start | bytes 786440 | tf_op jit(solution)/shard_map/while/body/eval_jaxpr/ppermute | solution.py:16
  255.8 9.0 %collective-permute-start.1 = (f32[4,128,128]{2,1,0:T(8,128)S(1)}, f32[4,128,128]{2,1,0:T(8,128)S(1)}, u32[]{:S(2)}, u32[]{:S(2)}) collective-permute-start(f32[4,128,128]{2,1,0:T(8,128)S(1)} %multiply_add_fusion.2), channel_id=1, source_target_pairs={{0,16},{16,32},{32,48},{48,64},{64,80},{80,96},{96,112},{112,128},... | collective-permute-start | bytes 786440 | tf_op jit(solution)/shard_map/while/body/eval_jaxpr/ppermute | solution.py:16
  264.9 9.0 %collective-permute-start.1 = (f32[4,128,128]{2,1,0:T(8,128)S(1)}, f32[4,128,128]{2,1,0:T(8,128)S(1)}, u32[]{:S(2)}, u32[]{:S(2)}) collective-permute-start(f32[4,128,128]{2,1,0:T(8,128)S(1)} %multiply_add_fusion.2), channel_id=1, source_target_pairs={{0,16},{16,32},{32,48},{48,64},{64,80},{80,96},{96,112},{112,128},... | collective-permute-start | bytes 786440 | tf_op jit(solution)/shard_map/while/body/eval_jaxpr/ppermute | solution.py:16
  273.9 9.0 %collective-permute-start.1 = (f32[4,128,128]{2,1,0:T(8,128)S(1)}, f32[4,128,128]{2,1,0:T(8,128)S(1)}, u32[]{:S(2)}, u32[]{:S(2)}) collective-permute-start(f32[4,128,128]{2,1,0:T(8,128)S(1)} %multiply_add_fusion.2), channel_id=1, source_target_pairs={{0,16},{16,32},{32,48},{48,64},{64,80},{80,96},{96,112},{112,128},... | collective-permute-start | bytes 786440 | tf_op jit(solution)/shard_map/while/body/eval_jaxpr/ppermute | solution.py:16
  283.0 9.0 %collective-permute-start.1 = (f32[4,128,128]{2,1,0:T(8,128)S(1)}, f32[4,128,128]{2,1,0:T(8,128)S(1)}, u32[]{:S(2)}, u32[]{:S(2)}) collective-permute-start(f32[4,128,128]{2,1,0:T(8,128)S(1)} %multiply_add_fusion.2), channel_id=1, source_target_pairs={{0,16},{16,32},{32,48},{48,64},{64,80},{80,96},{96,112},{112,128},... | collective-permute-start | bytes 786440 | tf_op jit(solution)/shard_map/while/body/eval_jaxpr/ppermute | solution.py:16
  292.1 9.0 %collective-permute-start.1 = (f32[4,128,128]{2,1,0:T(8,128)S(1)}, f32[4,128,128]{2,1,0:T(8,128)S(1)}, u32[]{:S(2)}, u32[]{:S(2)}) collective-permute-start(f32[4,128,128]{2,1,0:T(8,128)S(1)} %multiply_add_fusion.2), channel_id=1, source_target_pairs={{0,16},{16,32},{32,48},{48,64},{64,80},{80,96},{96,112},{112,128},... | collective-permute-start | bytes 786440 | tf_op jit(solution)/shard_map/while/body/eval_jaxpr/ppermute | solution.py:16
  302.0 186.5 %reduce-scatter.4.cloned.1.call-start = ((), (), s32[]{:S(2)}) async-start(), calls=%async_computation.3 | async-start | bytes 3342336
  (21 other events, 1311.4 us)
Sparse Core Ops, SparseCore 0:
  10.1 82.4 all-gather.3
  302.1 93.9 all-gather.5
  400.3 88.1 reduce-scatter.3
